TPU v7x, 32 devices: a whole 2x2x4 slice. The times are simulated.
32 devices in a mesh: row: 4 (over y, x), col: 8 (over z, core).
Axes of the slice: x: 2, y: 2, z: 4, core: 2. Of those that a mesh axis runs over, the one named last changes fastest.
Arguments:
- left_matrix: bfloat16 [3072, 32768], P('row', 'col'), may hold values from -6 to 6
- right_matrix: bfloat16 [32768, 4096], P('row', 'col'), may hold values from -0.0546875 to 0.0546875
- left_mask: int32 [24, 256], P('row', 'col'), may hold values from 0 to 1
- right_mask: int32 [256, 32], P('row', 'col'), may hold values from 0 to 1
- keep_mask: int32 [24, 32], P('row', 'col'), may hold values 0 or 1
Outputs:
- product: bfloat16 [3072, 4096], P('row', 'col')
All inputs are finite; a program needn't handle non-finite values. No bound on the sum of `keep_mask` on one device may be relied on, other than what follows from the above.
Results may differ from a plain program's by a relative error of at most 0.001.
Values may be sent and summed in bfloat16 or wider, within the bound.
A program may use at most 128 MiB of HBM per device.

v0:
```python
import jax
import jax.numpy as jnp
from jax import lax
from jax.sharding import PartitionSpec as P

BLOCK = 128
TICKS = 3


def passed_along(value, axis, by):
    length = lax.axis_size(axis)
    return lax.ppermute(value, axis, [(i, (i + by) % length) for i in range(length)])


def partner(block, axis, stride):
    count = lax.axis_size(axis)
    route = []
    for low in range(count):
        high = low | 1 << stride
        if high != low and high < count:
            route += [(low, high), (high, low)]
    return lax.ppermute(block, axis, route)


def sparsify(matrix, mask):
    rows, cols = matrix.shape
    shaped = matrix.reshape(rows // BLOCK, BLOCK, cols // BLOCK, BLOCK)
    return (shaped * mask[:, None, :, None].astype(matrix.dtype)).reshape(rows, cols)


def shards(left_matrix, right_matrix, left_mask, right_mask, keep_mask):
    row_index = lax.axis_index("row")
    col_index = lax.axis_index("col")
    group = col_index // 2
    parity = col_index % 2
    levels = lax.axis_size("row").bit_length() - 1
    left_sparse = sparsify(left_matrix, left_mask)
    right_sparse = sparsify(right_matrix, right_mask)

    def join(own, other):
        lower = jnp.where(parity == 0, own, other)
        upper = jnp.where(parity == 0, other, own)
        return jnp.concatenate([lower, upper], axis=1)

    for level in range(levels):
        moved = passed_along(right_sparse, "row", -(1 << level))
        right_sparse = jnp.where((group >> level) % 2 == 1, moved, right_sparse)
    holding = left_sparse
    for level in range(levels):
        moved = passed_along(holding, "col", -(2 << level))
        holding = jnp.where((row_index >> level) % 2 == 1, moved, holding)

    def whole(state):
        return join(state, partner(state, "col", 0))

    total = jnp.dot(whole(holding), right_sparse, preferred_element_type=jnp.float32)
    for tick in range(1, TICKS):
        holding = passed_along(holding, "col", -2)
        right_sparse = passed_along(right_sparse, "row", -1)
        total = total + jnp.dot(whole(holding), right_sparse, preferred_element_type=jnp.float32)
    rows, cols = total.shape
    kept = total.reshape(rows // BLOCK, BLOCK, cols // BLOCK, BLOCK) * keep_mask[
        :, None, :, None
    ].astype(jnp.float32)
    return kept.reshape(rows, cols).astype(jnp.bfloat16)


def solution(mesh):
    placed = (P("row", "col"), P("row", "col"), P("row", "col"), P("row", "col"), P("row", "col"))
    return jax.shard_map(
        shards, mesh=mesh, in_specs=placed, out_specs=P("row", "col"), check_vma=False
    )
```

profile of v0, /device:TPU:3, one launch (start us, length us, event | category | flops | bytes accessed | tf_op | source)
XLA Modules:
  0.0 835.0 jit_solution(3520347197175910123)
XLA Ops:
  0.8 5.5 mul.36
  6.3 9.6 %bitcast_multiply_fusion = bf16[8192,512]{1,0:T(8,128)(2,1)} fusion(bf16[8192,512]{1,0:T(8,128)(2,1)} %param.6, bf16[1024,8,4,128]{3,2,1,0:T(4,128)(2,1)} %bitcast.17), kind=kLoop, calls=%fused_computation.12 | loop fusion | flops 4194304 | bytes 25165824 | tf_op jit(solution)/shard_map/mul | solution.py:28
  16.8 7.5 bitcast_multiply_fusion.1
  24.2 3.6 collective-permute-start
  27.8 134.2 %collective-permute-done = bf16[768,4096]{1,0:T(8,128)(2,1)} collective-permute-done((bf16[768,4096]{1,0:T(8,128)(2,1)}, bf16[768,4096]{1,0:T(8,128)(2,1)}, u32[]{:S(2)}, u32[]{:S(2)}) %collective-permute-start) | collective-permute-done | bytes 6291488 | tf_op jit(solution)/shard_map/ppermute | solution.py:12
  162.1 6.0 broadcast_select_fusion.2
  169.3 29.2 %collective-permute-done.3 = bf16[8192,512]{1,0:T(8,128)(2,1)} collective-permute-done((bf16[8192,512]{1,0:T(8,128)(2,1)}, bf16[8192,512]{1,0:T(8,128)(2,1)}, u32[]{:S(2)}, u32[]{:S(2)}) %collective-permute-start.3) | collective-permute-done | bytes 8388640 | tf_op jit(solution)/shard_map/ppermute | solution.py:12
  198.4 7.2 broadcast_select_fusion
  206.9 233.0 %collective-permute-done.1 = bf16[768,4096]{1,0:T(8,128)(2,1)} collective-permute-done((bf16[768,4096]{1,0:T(8,128)(2,1)}, bf16[768,4096]{1,0:T(8,128)(2,1)}, u32[]{:S(2)}, u32[]{:S(2)}) %collective-permute-start.1) | collective-permute-done | bytes 6291488 | tf_op jit(solution)/shard_map/ppermute | solution.py:12
  439.9 6.0 broadcast_select_fusion.3
  445.9 3.7 collective-permute-start.5
  449.7 4.4 broadcast_select_fusion.1
  454.1 3.2 copy-done
  459.5 124.8 %collective-permute-done.5 = bf16[768,4096]{1,0:T(8,128)(2,1)} collective-permute-done((bf16[768,4096]{1,0:T(8,128)(2,1)}, bf16[768,4096]{1,0:T(8,128)(2,1)}, u32[]{:S(2)}, u32[]{:S(2)}) %collective-permute-start.5) | collective-permute-done | bytes 6291488 | tf_op jit(solution)/shard_map/ppermute | solution.py:12
  584.4 4.0 collective-permute-start.8
  590.0 49.6 %collective-permute-done.7 = bf16[8192,512]{1,0:T(8,128)(2,1)} collective-permute-done((bf16[8192,512]{1,0:T(8,128)(2,1)S(1)}, bf16[8192,512]{1,0:T(8,128)(2,1)}, u32[]{:S(2)}, u32[]{:S(2)}) %collective-permute-start.7) | collective-permute-done | bytes 8388640 | tf_op jit(solution)/shard_map/ppermute | solution.py:12
  641.0 81.2 %collective-permute-done.8 = bf16[768,4096]{1,0:T(8,128)(2,1)} collective-permute-done((bf16[768,4096]{1,0:T(8,128)(2,1)}, bf16[768,4096]{1,0:T(8,128)(2,1)}, u32[]{:S(2)}, u32[]{:S(2)}) %collective-permute-start.8) | collective-permute-done | bytes 6291488 | tf_op jit(solution)/shard_map/ppermute | solution.py:12
  724.4 5.2 broadcast_select_fusion.9
  729.6 11.1 %fusion = f32[768,512]{1,0:T(8,128)} fusion(bf16[8192,512]{1,0:T(8,128)(2,1)} %copy-done, bf16[768,4096]{1,0:T(8,128)(2,1)S(1)} %get-tuple-element.10, bf16[768,4096]{1,0:T(8,128)(2,1)S(1)} %get-tuple-element.9), kind=kOutput, calls=%fused_computation | convolution fusion | flops 6467616768 | bytes 22544384 | tf_op jit(solution)/shard_map/dot_general | solution.py:56
  740.8 5.2 broadcast_select_fusion.7
  746.0 11.2 %fusion.4 = f32[768,512]{1,0:T(8,128)} fusion(bf16[8192,512]{1,0:T(8,128)(2,1)} %collective-permute-done.7, bf16[768,4096]{1,0:T(8,128)(2,1)S(1)} %get-tuple-element.8, bf16[768,4096]{1,0:T(8,128)(2,1)S(1)} %get-tuple-element.7), kind=kOutput, calls=%fused_computation.4 | convolution fusion | flops 6467616768 | bytes 22544384 | tf_op jit(solution)/shard_map/dot_general | solution.py:60
  757.2 3.8 broadcast_select_fusion.5
  761.0 60.2 %collective-permute-done.10 = bf16[8192,512]{1,0:T(8,128)(2,1)} collective-permute-done((bf16[8192,512]{1,0:T(8,128)(2,1)}, bf16[8192,512]{1,0:T(8,128)(2,1)}, u32[]{:S(2)}, u32[]{:S(2)}) %collective-permute-start.10) | collective-permute-done | bytes 8388640 | tf_op jit(solution)/shard_map/ppermute | solution.py:12
  822.6 12.4 %fusion.12 = bf16[768,512]{1,0:T(8,128)(2,1)} fusion(f32[96,8,4,128]{3,2,1,0:T(4,128)} %bitcast.19, f32[768,512]{1,0:T(8,128)} %fusion, f32[768,512]{1,0:T(8,128)} %fusion.4, bf16[8192,512]{1,0:T(8,128)(2,1)} %collective-permute-done.10, bf16[768,4096]{1,0:T(8,128)(2,1)S(1)} %get-tuple-element.6, bf16[768,4096]{1,0:T(8,128)(2,1)S(1)} %get-tuple-element.5), kind=kOutput, calls=%fused_computation.25 | convolution fusion | flops 6469189632 | bytes 26476544 | tf_op jit(solution)/shard_map/dot_general | solution.py:60
  (24 shorter events, 12.9 us)
Async XLA Ops:
  6.3 9.6 %copy-start.1 = (s32[6,32]{1,0:T(8,128)S(1)}, s32[6,32]{1,0:T(8,128)}, u32[]{:S(2)}) copy-start(s32[6,32]{1,0:T(8,128)} %param.7) | copy-start | bytes 2308
  15.9 182.6 %collective-permute-start.3 = (bf16[8192,512]{1,0:T(8,128)(2,1)}, bf16[8192,512]{1,0:T(8,128)(2,1)}, u32[]{:S(2)}, u32[]{:S(2)}) collective-permute-start(bf16[8192,512]{1,0:T(8,128)(2,1)} %bitcast_multiply_fusion), channel_id=1, source_target_pairs={{0,24},{8,0},{16,8},{24,16},{1,25},{9,1},{17,9},{25,17},{2,26},{10... | collective-permute-start | bytes 25165832 | tf_op jit(solution)/shard_map/ppermute | solution.py:12
  24.2 137.8 %collective-permute-start = (bf16[768,4096]{1,0:T(8,128)(2,1)}, bf16[768,4096]{1,0:T(8,128)(2,1)}, u32[]{:S(2)}, u32[]{:S(2)}) collective-permute-start(bf16[768,4096]{1,0:T(8,128)(2,1)} %bitcast_multiply_fusion.1), channel_id=1, source_target_pairs={{0,6},{1,7},{2,0},{3,1},{4,2},{5,3},{6,4},{7,5},{8,14},{9,15},{10,... | collective-permute-start | bytes 18874376 | tf_op jit(solution)/shard_map/ppermute | solution.py:12
  168.1 271.8 %collective-permute-start.1 = (bf16[768,4096]{1,0:T(8,128)(2,1)}, bf16[768,4096]{1,0:T(8,128)(2,1)}, u32[]{:S(2)}, u32[]{:S(2)}) collective-permute-start(bf16[768,4096]{1,0:T(8,128)(2,1)} %broadcast_select_fusion.2), channel_id=1, source_target_pairs={{0,4},{1,5},{2,6},{3,7},{4,0},{5,1},{6,2},{7,3},{8,12},{9,13},{10,... | collective-permute-start | bytes 18874376 | tf_op jit(solution)/shard_map/ppermute | solution.py:12
  205.7 244.0 %collective-permute-start.4 = (bf16[8192,512]{1,0:T(8,128)(2,1)}, bf16[8192,512]{1,0:T(8,128)(2,1)}, u32[]{:S(2)}, u32[]{:S(2)}) collective-permute-start(bf16[8192,512]{1,0:T(8,128)(2,1)} %broadcast_select_fusion), channel_id=1, source_target_pairs={{0,16},{8,24},{16,0},{24,8},{1,17},{9,25},{17,1},{25,9},{2,18},{10... | collective-permute-start | bytes 25165832 | tf_op jit(solution)/shard_map/ppermute | solution.py:12
  445.9 138.4 %collective-permute-start.5 = (bf16[768,4096]{1,0:T(8,128)(2,1)}, bf16[768,4096]{1,0:T(8,128)(2,1)}, u32[]{:S(2)}, u32[]{:S(2)}) collective-permute-start(bf16[768,4096]{1,0:T(8,128)(2,1)} %broadcast_select_fusion.3), channel_id=1, source_target_pairs={{0,6},{1,7},{2,0},{3,1},{4,2},{5,3},{6,4},{7,5},{8,14},{9,15},{10,... | collective-permute-start | bytes 18874376 | tf_op jit(solution)/shard_map/ppermute | solution.py:12
  449.7 191.2 %copy-start.2 = (s32[6,4]{0,1:T(4,128)S(1)}, s32[6,4]{0,1:T(4,128)}, u32[]{:S(2)}) copy-start(s32[6,4]{0,1:T(4,128)} %param.9) | copy-start | bytes 292
  454.1 3.2 copy-start
  457.3 182.2 %collective-permute-start.7 = (bf16[8192,512]{1,0:T(8,128)(2,1)S(1)}, bf16[8192,512]{1,0:T(8,128)(2,1)}, u32[]{:S(2)}, u32[]{:S(2)}) collective-permute-start(bf16[8192,512]{1,0:T(8,128)(2,1)S(1)} %broadcast_select_fusion.1), channel_id=1, source_target_pairs={{0,24},{8,0},{16,8},{24,16},{1,25},{9,1},{17,9},{25,17},{2,26},{10... | collective-permute-start | bytes 25165832 | tf_op jit(solution)/shard_map/ppermute | solution.py:12
  584.4 137.8 %collective-permute-start.8 = (bf16[768,4096]{1,0:T(8,128)(2,1)}, bf16[768,4096]{1,0:T(8,128)(2,1)}, u32[]{:S(2)}, u32[]{:S(2)}) collective-permute-start(bf16[768,4096]{1,0:T(8,128)(2,1)} %collective-permute-done.5), channel_id=1, source_target_pairs={{0,6},{1,7},{2,0},{3,1},{4,2},{5,3},{6,4},{7,5},{8,14},{9,15},{10,... | collective-permute-start | bytes 18874376 | tf_op jit(solution)/shard_map/ppermute | solution.py:12
  588.4 136.0 %collective-permute-start.2 = (bf16[768,4096]{1,0:T(8,128)(2,1)}, bf16[768,4096]{1,0:T(8,128)(2,1)}, u32[]{:S(2)}, u32[]{:S(2)}) collective-permute-start(bf16[768,4096]{1,0:T(8,128)(2,1)} %broadcast_select_fusion.3), channel_id=1, source_target_pairs={{0,1},{1,0},{2,3},{3,2},{4,5},{5,4},{6,7},{7,6},{8,9},{9,8},{10,11... | collective-permute-start | bytes 18874376 | tf_op jit(solution)/shard_map/ppermute | solution.py:22
  590.0 150.8 %collective-permute-start.6 = (bf16[768,4096]{1,0:T(8,128)(2,1)}, bf16[768,4096]{1,0:T(8,128)(2,1)}, u32[]{:S(2)}, u32[]{:S(2)}) collective-permute-start(bf16[768,4096]{1,0:T(8,128)(2,1)} %collective-permute-done.5), channel_id=1, source_target_pairs={{0,1},{1,0},{2,3},{3,2},{4,5},{5,4},{6,7},{7,6},{8,9},{9,8},{10,11... | collective-permute-start | bytes 18874376 | tf_op jit(solution)/shard_map/ppermute | solution.py:22
  639.6 181.6 %collective-permute-start.10 = (bf16[8192,512]{1,0:T(8,128)(2,1)}, bf16[8192,512]{1,0:T(8,128)(2,1)}, u32[]{:S(2)}, u32[]{:S(2)}) collective-permute-start(bf16[8192,512]{1,0:T(8,128)(2,1)} %collective-permute-done.7), channel_id=1, source_target_pairs={{0,24},{8,0},{16,8},{24,16},{1,25},{9,1},{17,9},{25,17},{2,26},{10... | collective-permute-start | bytes 25165832 | tf_op jit(solution)/shard_map/ppermute | solution.py:12
  722.2 35.0 %collective-permute-start.9 = (bf16[768,4096]{1,0:T(8,128)(2,1)}, bf16[768,4096]{1,0:T(8,128)(2,1)S(1)}, u32[]{:S(2)}, u32[]{:S(2)}) collective-permute-start(bf16[768,4096]{1,0:T(8,128)(2,1)} %collective-permute-done.8), channel_id=1, source_target_pairs={{0,1},{1,0},{2,3},{3,2},{4,5},{5,4},{6,7},{7,6},{8,9},{9,8},{10,11... | collective-permute-start | bytes 18874376 | tf_op jit(solution)/shard_map/ppermute | solution.py:22
where the time goes:
time: 839 us; the launch traced here: 835 us
  waiting for transfers between devices  712 us (85%)
  other arithmetic  55.8 us (7%)
  matrix products  34.7 us (4%)
  starting transfers between devices  21 us (3%)
  local copies, waits for them, and re-layouts  11.2 us (1%)
    ppermute x8, waiting for transfers between devices, passed_along(): lax.ppermute(value, axis, [(i, (i + by) % length) for i in range(length)])  712 us
    dot_general x3, matrix products, shards(): jnp.dot(whole(holding), right_sparse, preferred_element_type=jnp.float32)  34.7 us
    ppermute x8, starting transfers between devices, passed_along(): lax.ppermute(value, axis, [(i, (i + by) % length) for i in range(length)])  17.2 us
    mul x2, other arithmetic, sparsify(): shaped * mask[:, None, :, None].astype(matrix.dtype)  17.1 us
  transfers between devices with their start and end apart: 11, of which 7 were waited for; matrix products, arithmetic and copies ran while one was open for 8% of the time, Pallas kernels for 0%

commit v1 on v0

--- a/solution.py
+++ b/solution.py
@@ -1,6 +1,10 @@
+import functools
+
 import jax
 import jax.numpy as jnp
 from jax import lax
+from jax.experimental import pallas as pl
+from jax.experimental.pallas import tpu as pltpu
 from jax.sharding import PartitionSpec as P
 
 BLOCK = 128
@@ -65,8 +69,233 @@
     return kept.reshape(rows, cols).astype(jnp.bfloat16)
 
 
+LEFT_PIECES = 4
+RIGHT_PIECES = 4
+SUM_PIECES = 4
+
+
+def product_kernel(lsrc, rsrc, out, lbuf, rbuf, acc, core_sum, far_sum, loc, y_l, y_r, x_own, x_fwd, z_one, z_two, swap, sums):
+    r, c = lax.axis_index("row"), lax.axis_index("col")
+    y, x = r // 2, lax.rem(r, 2)
+    z, p = c // 2, lax.rem(c, 2)
+    rows, half = lbuf.shape[2:]
+    width = rbuf.shape[3]
+    lrows, rrows, srows = rows // LEFT_PIECES, half // RIGHT_PIECES, rows // SUM_PIECES
+    ring = lbuf.shape[1]
+
+    def device(dy, dx, dz, core):
+        ny = 1 - y if dy else y
+        nx = 1 - x if dx else x
+        return (ny * 2 + nx, lax.rem(z + dz + ring, ring) * 2 + core)
+
+    def unit_of(dy, dx):
+        return (1 - y if dy else y) * 2 + (1 - x if dx else x)
+
+    def copy(src, dst, sems, index, to):
+        send, recv = sems
+        return pltpu.make_async_remote_copy(
+            src_ref=src, dst_ref=dst, send_sem=send.at[index], recv_sem=recv.at[index],
+            device_id=to, device_id_type=pl.DeviceIdType.MESH)
+
+    def arrived(dst, sems, index):
+        copy(dst, dst, sems, index, device(0, 0, 0, 1 - p)).wait_recv()
+
+    def used(panel, unit):
+        return lax.rem(unit - (x + 2 * panel) - z + 2 * ring, ring) < TICKS
+
+    barrier = pltpu.get_barrier_semaphore()
+    peers = [device(1, 0, 0, 0), device(1, 0, 0, 1), device(0, 1, 0, 0), device(0, 1, 0, 1),
+             device(0, 0, 0, 1 - p), device(0, 0, 1, p), device(0, 0, -1, p)]
+    for peer in peers:
+        pl.semaphore_signal(barrier, inc=1, device_id=peer, device_id_type=pl.DeviceIdType.MESH)
+    pl.semaphore_wait(barrier, len(peers))
+
+    pending = []
+
+    def send(transfer, when=None):
+        pending.append((transfer, when))
+        if when is None:
+            transfer.start()
+        else:
+            @pl.when(when)
+            def _():
+                transfer.start()
+
+    def left_at(panel, unit, j):
+        return lbuf.at[panel, unit, pl.ds(j * lrows, lrows)]
+
+    def right_at(unit, q, j):
+        return rbuf.at[unit, q, pl.ds(j * rrows, rrows)]
+
+    def left_source(part, j):
+        return lsrc.at[pl.ds(j * lrows, lrows), pl.ds(pl.multiple_of(part * half, 128), half)]
+
+    def right_source(core, part, j):
+        return rsrc.at[pl.ds(pl.multiple_of((core * 2 + part) * half + j * rrows, 128), rrows)]
+
+    first = {}
+    first[0, -1] = True
+    first[1, -1] = x == 1
+    first[0, 1] = x == 1
+    first[1, 1] = True
+
+    def first_hop(panel_is_own, j):
+        panel = y if panel_is_own else 1 - y
+        for d in (-1, 1):
+            ok = (panel == (0 if d == -1 else 1)) | (x == 1)
+            src = left_source(y, j) if panel_is_own else left_at(panel, z, j)
+            n = (0 if d == -1 else 1, 0 if panel_is_own else 1, j)
+            sem = (0 if d == -1 else 1, panel, j)
+            send(copy(src, left_at(panel, z, j), z_one, sem, device(0, 0, d, p)), ok)
+
+    own_left = [pltpu.make_async_copy(lsrc.at[:, pl.ds(pl.multiple_of(y * half, 128), half)], lbuf.at[y, z], loc.at[0]),
+                pltpu.make_async_copy(rsrc.at[pl.ds(pl.multiple_of((p * 2 + y) * half, 128), half)], rbuf.at[r, p], loc.at[1])]
+    for j in range(LEFT_PIECES):
+        send(copy(left_source(1 - y, j), left_at(y, z, j), y_l, (j,), device(1, 0, 0, p)))
+        first_hop(True, j)
+        if j < RIGHT_PIECES:
+            for core in range(2):
+                send(copy(right_source(core, y, j), right_at(r, p, j), x_own, (core, p, j), device(0, 1, 0, core)))
+    send(copy(rsrc.at[pl.ds(pl.multiple_of(((1 - p) * 2 + y) * half, 128), half)], rbuf.at[r, p], swap, (0,), device(0, 0, 0, 1 - p)))
+    for local in own_left:
+        local.start()
+    for j in range(RIGHT_PIECES):
+        for core in range(2):
+            send(copy(right_source(core, 1 - y, j), right_at(r, p, j), y_r, (core, p, j), device(1, 0, 0, core)))
+
+    acc[...] = jnp.zeros_like(acc)
+
+    def one_hop_arrives(panel, d, j):
+        unit = lax.rem(z - d + ring, ring)
+        ok = (panel == (0 if d == -1 else 1)) | (x == 1)
+        @pl.when(ok)
+        def _():
+            arrived(left_at(panel, unit, j), z_one, (0 if d == -1 else 1, panel, j))
+        mine = j < LEFT_PIECES // 2 if d == -1 else j >= LEFT_PIECES // 2
+        on = jnp.where(x == 0, panel == (0 if d == -1 else 1), (panel == 0) & mine)
+        send(copy(left_at(panel, unit, j), left_at(panel, unit, j), z_two, (panel, j), device(0, 0, d, p)), on)
+
+    for j in range(LEFT_PIECES):
+        arrived(left_at(1 - y, z, j), y_l, (j,))
+        first_hop(False, j)
+        for d in (-1, 1):
+            one_hop_arrives(y, d, j)
+    behind = unit_of(1, 0)
+
+    for j in range(max(LEFT_PIECES, RIGHT_PIECES)):
+        if j < LEFT_PIECES:
+            for d in (-1, 1):
+                one_hop_arrives(1 - y, d, j)
+        if j < RIGHT_PIECES:
+            for q in range(2):
+                arrived(right_at(behind, q, j), y_r, (p, q, j))
+                send(copy(right_at(behind, q, j), right_at(behind, q, j), x_fwd, (q, j), device(0, 1, 0, p)))
+
+    def multiply(panel, unit, start, depth):
+        @pl.when(used(panel, unit))
+        def _():
+            for q in range(2):
+                acc[panel, q] += jnp.dot(
+                    lbuf[panel, unit, :, start:start + depth], rbuf[unit, q, start:start + depth],
+                    preferred_element_type=jnp.float32)
+
+    for local in own_left:
+        local.wait()
+    arrived(rbuf.at[r, 1 - p], swap, (0,))
+    across = unit_of(0, 1)
+    for j in range(RIGHT_PIECES):
+        for q in range(2):
+            arrived(right_at(across, q, j), x_own, (p, q, j))
+    opposite = lax.rem(z + 2, ring)
+    for panel in range(2):
+        for j in range(LEFT_PIECES):
+            @pl.when((x == 0) | (panel == 0))
+            def _():
+                arrived(left_at(panel, opposite, j), z_two, (panel, j))
+
+    def early(panel):
+        @pl.loop(0, 3)
+        def _(step):
+            unit = jnp.where(step == 0, r, jnp.where(step == 1, across, behind))
+            multiply(panel, unit, 0, half)
+
+    early(1 - y)
+    last = unit_of(1, 1)
+    for j in range(RIGHT_PIECES):
+        for q in range(2):
+            arrived(right_at(last, q, j), x_fwd, (q, j))
+        multiply(1 - y, last, j * rrows, rrows)
+
+    def part(ref, j, *index):
+        return ref.at[(*index, pl.ds(j * srows, srows))]
+
+    for j in range(SUM_PIECES):
+        send(copy(part(acc, j, 1 - y, 1 - p), part(core_sum, j, 0), sums, (0, j), device(0, 0, 0, 1 - p)))
+    for j in range(SUM_PIECES):
+        piece = pl.ds(j * srows, srows)
+        arrived(part(core_sum, j, 0), sums, (0, j))
+        acc[1 - y, p, piece] += core_sum[0, piece]
+        send(copy(part(acc, j, 1 - y, p), part(far_sum, j), sums, (1, j), device(1, 0, 0, p)))
+    early(y)
+    multiply(y, last, 0, half)
+    for j in range(SUM_PIECES):
+        send(copy(part(acc, j, y, 1 - p), part(core_sum, j, 1), sums, (2, j), device(0, 0, 0, 1 - p)))
+    for j in range(SUM_PIECES):
+        piece = pl.ds(j * srows, srows)
+        arrived(part(core_sum, j, 1), sums, (2, j))
+        arrived(part(far_sum, j), sums, (1, j))
+        out[piece] = acc[y, p, piece] + core_sum[1, piece] + far_sum[piece]
+
+    for transfer, when in pending:
+        if when is None:
+            transfer.wait_send()
+        else:
+            @pl.when(when)
+            def _():
+                transfer.wait_send()
+
+
+def kernel_entry(sems, lsrc, rsrc, out, lbuf, rbuf, acc, core_sum, far_sum, loc, *rest):
+    pairs = [(rest[2 * i], rest[2 * i + 1]) for i in range(sems)]
+    product_kernel(lsrc, rsrc, out, lbuf, rbuf, acc, core_sum, far_sum, loc, *pairs)
+
+
+def split_shards(left_matrix, right_matrix, left_mask, right_mask, keep_mask):
+    left_sparse = sparsify(left_matrix, left_mask)
+    right_sparse = sparsify(right_matrix, right_mask)
+    rows, depth = left_matrix.shape
+    width = right_matrix.shape[1]
+    half = depth // 2
+    units = lax.axis_size("row")
+    shapes = [(LEFT_PIECES,), (2, 2, RIGHT_PIECES), (2, 2, RIGHT_PIECES), (2, RIGHT_PIECES),
+              (2, 2, LEFT_PIECES), (2, LEFT_PIECES), (1,), (3, SUM_PIECES)]
+    sems = [pltpu.SemaphoreType.DMA(shape) for shape in shapes for _ in range(2)]
+    total = pl.pallas_call(
+        functools.partial(kernel_entry, len(shapes)),
+        out_shape=jax.ShapeDtypeStruct((rows, width), jnp.float32),
+        in_specs=[pl.BlockSpec(memory_space=pl.ANY)] * 2,
+        out_specs=pl.BlockSpec(memory_space=pltpu.VMEM),
+        scratch_shapes=[
+            pltpu.VMEM((2, units, rows, half), jnp.bfloat16),
+            pltpu.VMEM((units, 2, half, width), jnp.bfloat16),
+            pltpu.VMEM((2, 2, rows, width), jnp.float32),
+            pltpu.VMEM((2, rows, width), jnp.float32),
+            pltpu.VMEM((rows, width), jnp.float32),
+            pltpu.SemaphoreType.DMA((2,)),
+            *sems,
+        ],
+        compiler_params=pltpu.CompilerParams(
+            collective_id=0, has_side_effects=True, vmem_limit_bytes=63 * 1024 * 1024),
+    )(left_sparse, right_sparse)
+    kept = total.reshape(rows // BLOCK, BLOCK, width // BLOCK, BLOCK) * keep_mask[
+        :, None, :, None
+    ].astype(jnp.float32)
+    return kept.reshape(rows, width).astype(jnp.bfloat16)
+
+
 def solution(mesh):
     placed = (P("row", "col"), P("row", "col"), P("row", "col"), P("row", "col"), P("row", "col"))
+    two_by_two = mesh.shape["row"] == TICKS + 1 and mesh.shape["col"] == 2 * mesh.shape["row"]
     return jax.shard_map(
-        shards, mesh=mesh, in_specs=placed, out_specs=P("row", "col"), check_vma=False
+        split_shards if two_by_two else shards, mesh=mesh, in_specs=placed, out_specs=P("row", "col"), check_vma=False
     )

time: 839 us -> 421 us (0.50)
  waiting for transfers between devices: 712 us -> 0 us
  Pallas kernels: 0 us -> 394 us
  other arithmetic: 55.8 us -> 20.4 us
  matrix products: 34.7 us -> 0 us
  starting transfers between devices: 21 us -> 0 us
    ppermute x11 -> x0, waiting for transfers between devices: 712 us -> none  [the longest x8 712 us: passed_along(): lax.ppermute(value, axis, [(i, (i + by) % length) for i in range(length)])]
    pallas_call x0 -> x1, Pallas kernels: none -> 394 us  [split_shards(): pl.pallas_call(functools.partial(kernel_entry, len(shapes)), out_shape=ja...]
    select_n x7 -> x0, other arithmetic: 38 us -> none  [the longest x3 14.3 us: join(): lower = jnp.where(parity == 0, own, other)]
    dot_general x3 -> x0, matrix products: 34.7 us -> none  [shards(): jnp.dot(whole(holding), right_sparse, preferred_element_type=jnp.float32)]
    ppermute x11 -> x0, starting transfers between devices: 21 us -> none  [the longest x8 17.2 us: passed_along(): lax.ppermute(value, axis, [(i, (i + by) % length) for i in range(length)])]
  transfers between devices with their start and end apart: 11 -> 0, of which waited for: 7 -> 0; matrix products, arithmetic and copies ran while one was open for 8% -> 0% of each run, Pallas kernels for 0% -> 0%
where the time goes in v1:
time: 421 us
  Pallas kernels  394 us (94%)
  other arithmetic  20.4 us (5%)
  local copies, waits for them, and re-layouts  6.81 us (2%)
    pallas_call x1, Pallas kernels, split_shards(): pl.pallas_call(functools.partial(kernel_entry, len(shapes)), out_shape=ja...  394 us
    mul x2, other arithmetic, sparsify(): shaped * mask[:, None, :, None].astype(matrix.dtype)  17.2 us

profile of v1, /device:TPU:3, one launch (start us, length us, event | category | flops | bytes accessed | tf_op | source)
XLA Modules:
  0.0 420.8 jit_solution(12228539254607204105)
XLA Ops:
  0.0 0.7 convert_element_type.16
  0.7 0.1 copy.6
  0.8 5.4 %mul.36 = bf16[64,128,4,128]{3,2,1,0:T(4,128)(2,1)} broadcast(bf16[64,4]{1,0:T(8,128)(2,1)S(1)} %copy.6), dimensions={0,2} | broadcast | bytes 8389120 | tf_op jit(solution)/shard_map/mul | solution.py:32
  6.2 0.0 copy-start
  6.2 9.6 %bitcast_multiply_fusion.rsrc = bf16[8192,512]{1,0:T(8,128)(2,1)} fusion(bf16[8192,512]{1,0:T(8,128)(2,1)} %param.6, bf16[1024,8,4,128]{3,2,1,0:T(4,128)(2,1)} %bitcast.14), kind=kLoop, calls=%fused_computation | loop fusion | flops 4194304 | bytes 25165824 | tf_op jit(solution)/shard_map/mul | solution.py:32
  15.8 0.0 copy-done
  15.9 0.9 mul.33
  16.7 7.6 %bitcast_multiply_fusion.1.lsrc = bf16[768,4096]{1,0:T(8,128)(2,1)} fusion(bf16[768,4096]{1,0:T(8,128)(2,1)} %param.5, bf16[96,8,32,128]{3,2,1,0:T(8,128)(2,1)S(1)} %bitcast.15), kind=kLoop, calls=%fused_computation.1 | loop fusion | flops 3145728 | bytes 18874368 | tf_op jit(solution)/shard_map/mul | solution.py:32
  24.3 0.0 copy-start.1
  24.3 393.5 %shard_map.55 = f32[768,512]{1,0:T(8,128)} custom-call(bf16[768,4096]{1,0:T(8,128)(2,1)} %bitcast_multiply_fusion.1.lsrc, bf16[8192,512]{1,0:T(8,128)(2,1)} %bitcast_multiply_fusion.rsrc), custom_call_target="tpu_custom_call" | custom-call | tf_op jit(solution)/shard_map/pallas_call | solution.py:273
  417.8 0.0 copy-done.1
  417.9 0.1 copy.7
  418.0 0.3 mul.39
  418.2 2.5 fusion
  (2 shorter events, 0.0 us)
Async XLA Ops:
  6.2 9.6 %copy-start = (s32[6,32]{1,0:T(8,128)S(1)}, s32[6,32]{1,0:T(8,128)}, u32[]{:S(2)}) copy-start(s32[6,32]{1,0:T(8,128)} %param.7) | copy-start | bytes 2308
  24.3 393.5 %copy-start.1 = (s32[6,4]{0,1:T(4,128)S(1)}, s32[6,4]{0,1:T(4,128)}, u32[]{:S(2)}) copy-start(s32[6,4]{0,1:T(4,128)} %param.9) | copy-start | bytes 292

commit v2 on v1

--- a/solution.py
+++ b/solution.py
@@ -74,7 +74,7 @@
 SUM_PIECES = 4
 
 
-def product_kernel(lsrc, rsrc, out, lbuf, rbuf, acc, core_sum, far_sum, loc, y_l, y_r, x_own, x_fwd, z_one, z_two, swap, sums):
+def product_kernel(lsrc, rsrc, out, lbuf, rbuf, acc, core_sum, far_sum, via, loc, y_l, y_r, x_own, x_fwd, line, side, swap, sums):
     r, c = lax.axis_index("row"), lax.axis_index("col")
     y, x = r // 2, lax.rem(r, 2)
     z, p = c // 2, lax.rem(c, 2)
@@ -133,20 +133,75 @@
     def right_source(core, part, j):
         return rsrc.at[pl.ds(pl.multiple_of((core * 2 + part) * half + j * rrows, 128), rrows)]
 
-    first = {}
-    first[0, -1] = True
-    first[1, -1] = x == 1
-    first[0, 1] = x == 1
-    first[1, 1] = True
+    def needed(panel, d, at, unit):
+        ok = False
+        for step in range(ring):
+            spot = at + step * d
+            use = lax.rem(unit - (x + 2 * panel) - spot + 3 * ring, ring) < TICKS
+            ok = ok | ((spot >= 0) & (spot < ring) & use)
+        return ok & (unit >= 0) & (unit < ring)
+
+    def comes(panel, d, m):
+        return needed(panel, d, z, z - m * d) & (z - m * d >= 0) & (z - m * d < ring)
+
+    def leaves(panel, d, m):
+        return needed(panel, d, z + d, z - m * d) & ((m == 0) | comes(panel, d, m))
+
+    def slot(panel, d, m, j):
+        return (0 if d == -1 else 1, panel, m, j)
+
+    def unit_back(d, m):
+        return lax.clamp(0, z - m * d, ring - 1)
+
+    def aside(d, panel, j):
+        inner = ring - 2 if d == 1 else 1
+        return (panel == 0) & (z == inner) & (j >= LEFT_PIECES // 2)
 
     def first_hop(panel_is_own, j):
         panel = y if panel_is_own else 1 - y
-        for d in (-1, 1):
-            ok = (panel == (0 if d == -1 else 1)) | (x == 1)
-            src = left_source(y, j) if panel_is_own else left_at(panel, z, j)
-            n = (0 if d == -1 else 1, 0 if panel_is_own else 1, j)
-            sem = (0 if d == -1 else 1, panel, j)
-            send(copy(src, left_at(panel, z, j), z_one, sem, device(0, 0, d, p)), ok)
+        src = left_source(y, j) if panel_is_own else left_at(panel, z, j)
+        for d in (-1, 1):
+            go = leaves(panel, d, 0)
+            off = aside(d, panel, j) & (x == 1)
+            send(copy(src, left_at(panel, z, j), line, slot(panel, d, 0, j), device(0, 0, d, p)), go & ~off)
+            if j >= LEFT_PIECES // 2:
+                send(copy(src, via.at[j - LEFT_PIECES // 2], side, (0, j), device(0, 1, 0, p)), go & off)
+
+    def forward(panel, m, j):
+        for d in (-1, 1):
+            go = leaves(panel, d, m)
+            unit = unit_back(d, m)
+            @pl.when(go)
+            def _():
+                arrived(left_at(panel, unit, j), line, slot(panel, d, m - 1, j))
+            send(copy(left_at(panel, unit, j), left_at(panel, unit, j), line, slot(panel, d, m, j), device(0, 0, d, p)), go)
+
+    def settle(panel, m, j):
+        for d in (-1, 1):
+            @pl.when(comes(panel, d, m) & ~leaves(panel, d, m))
+            def _():
+                arrived(left_at(panel, unit_back(d, m), j), line, slot(panel, d, m - 1, j))
+
+    def detour(j):
+        hold = via.at[j - LEFT_PIECES // 2]
+        for d in (-1, 1):
+            inner = ring - 2 if d == 1 else 1
+            here = (x == 0) & (z == inner)
+            @pl.when(here)
+            def _():
+                arrived(hold, side, (0, j))
+            send(copy(hold, hold, side, (1, j), device(0, 0, d, p)), here)
+
+    def detour_back(j):
+        hold = via.at[j - LEFT_PIECES // 2]
+        for d in (-1, 1):
+            inner = ring - 2 if d == 1 else 1
+            end = inner + d
+            there = (x == 0) & (z == end)
+            @pl.when(there)
+            def _():
+                arrived(hold, side, (1, j))
+            send(copy(hold, left_at(0, inner, j), line, slot(0, d, 0, j), device(0, 1, 0, p)), there)
 
     own_left = [pltpu.make_async_copy(lsrc.at[:, pl.ds(pl.multiple_of(y * half, 128), half)], lbuf.at[y, z], loc.at[0]),
                 pltpu.make_async_copy(rsrc.at[pl.ds(pl.multiple_of((p * 2 + y) * half, 128), half)], rbuf.at[r, p], loc.at[1])]
@@ -165,31 +220,23 @@
 
     acc[...] = jnp.zeros_like(acc)
 
-    def one_hop_arrives(panel, d, j):
-        unit = lax.rem(z - d + ring, ring)
-        ok = (panel == (0 if d == -1 else 1)) | (x == 1)
-        @pl.when(ok)
-        def _():
-            arrived(left_at(panel, unit, j), z_one, (0 if d == -1 else 1, panel, j))
-        mine = j < LEFT_PIECES // 2 if d == -1 else j >= LEFT_PIECES // 2
-        on = jnp.where(x == 0, panel == (0 if d == -1 else 1), (panel == 0) & mine)
-        send(copy(left_at(panel, unit, j), left_at(panel, unit, j), z_two, (panel, j), device(0, 0, d, p)), on)
-
+    behind = unit_of(1, 0)
     for j in range(LEFT_PIECES):
         arrived(left_at(1 - y, z, j), y_l, (j,))
         first_hop(False, j)
-        for d in (-1, 1):
-            one_hop_arrives(y, d, j)
-    behind = unit_of(1, 0)
-
-    for j in range(max(LEFT_PIECES, RIGHT_PIECES)):
-        if j < LEFT_PIECES:
-            for d in (-1, 1):
-                one_hop_arrives(1 - y, d, j)
-        if j < RIGHT_PIECES:
-            for q in range(2):
-                arrived(right_at(behind, q, j), y_r, (p, q, j))
-                send(copy(right_at(behind, q, j), right_at(behind, q, j), x_fwd, (q, j), device(0, 1, 0, p)))
+    for j in range(LEFT_PIECES):
+        forward(1 - y, 1, j)
+    for j in range(LEFT_PIECES // 2, LEFT_PIECES):
+        detour(j)
+    for j in range(RIGHT_PIECES):
+        for q in range(2):
+            arrived(right_at(behind, q, j), y_r, (p, q, j))
+            send(copy(right_at(behind, q, j), right_at(behind, q, j), x_fwd, (q, j), device(0, 1, 0, p)))
+    for j in range(LEFT_PIECES // 2, LEFT_PIECES):
+        detour_back(j)
+    for m, own in ((2, False), (1, True), (2, True)):
+        for j in range(LEFT_PIECES):
+            forward(y if own else 1 - y, m, j)
 
     def multiply(panel, unit, start, depth):
         @pl.when(used(panel, unit))
@@ -206,12 +253,9 @@
     for j in range(RIGHT_PIECES):
         for q in range(2):
             arrived(right_at(across, q, j), x_own, (p, q, j))
-    opposite = lax.rem(z + 2, ring)
-    for panel in range(2):
+    for m in range(1, ring):
         for j in range(LEFT_PIECES):
-            @pl.when((x == 0) | (panel == 0))
-            def _():
-                arrived(left_at(panel, opposite, j), z_two, (panel, j))
+            settle(1 - y, m, j)
 
     def early(panel):
         @pl.loop(0, 3)
@@ -236,8 +280,14 @@
         arrived(part(core_sum, j, 0), sums, (0, j))
         acc[1 - y, p, piece] += core_sum[0, piece]
         send(copy(part(acc, j, 1 - y, p), part(far_sum, j), sums, (1, j), device(1, 0, 0, p)))
-    early(y)
-    multiply(y, last, 0, half)
+    multiply(y, z, 0, half)
+    for m in range(1, ring):
+        for j in range(LEFT_PIECES):
+            settle(y, m, j)
+        for d in (-1, 1):
+            @pl.when((z - m * d >= 0) & (z - m * d < ring))
+            def _():
+                multiply(y, unit_back(d, m), 0, half)
     for j in range(SUM_PIECES):
         send(copy(part(acc, j, y, 1 - p), part(core_sum, j, 1), sums, (2, j), device(0, 0, 0, 1 - p)))
     for j in range(SUM_PIECES):
@@ -255,9 +305,9 @@
                 transfer.wait_send()
 
 
-def kernel_entry(sems, lsrc, rsrc, out, lbuf, rbuf, acc, core_sum, far_sum, loc, *rest):
+def kernel_entry(sems, lsrc, rsrc, out, lbuf, rbuf, acc, core_sum, far_sum, via, loc, *rest):
     pairs = [(rest[2 * i], rest[2 * i + 1]) for i in range(sems)]
-    product_kernel(lsrc, rsrc, out, lbuf, rbuf, acc, core_sum, far_sum, loc, *pairs)
+    product_kernel(lsrc, rsrc, out, lbuf, rbuf, acc, core_sum, far_sum, via, loc, *pairs)
 
 
 def split_shards(left_matrix, right_matrix, left_mask, right_mask, keep_mask):
@@ -268,7 +318,7 @@
     half = depth // 2
     units = lax.axis_size("row")
     shapes = [(LEFT_PIECES,), (2, 2, RIGHT_PIECES), (2, 2, RIGHT_PIECES), (2, RIGHT_PIECES),
-              (2, 2, LEFT_PIECES), (2, LEFT_PIECES), (1,), (3, SUM_PIECES)]
+              (2, 2, units - 1, LEFT_PIECES), (2, LEFT_PIECES), (1,), (3, SUM_PIECES)]
     sems = [pltpu.SemaphoreType.DMA(shape) for shape in shapes for _ in range(2)]
     total = pl.pallas_call(
         functools.partial(kernel_entry, len(shapes)),
@@ -281,6 +331,7 @@
             pltpu.VMEM((2, 2, rows, width), jnp.float32),
             pltpu.VMEM((2, rows, width), jnp.float32),
             pltpu.VMEM((rows, width), jnp.float32),
+            pltpu.VMEM((LEFT_PIECES // 2, rows // LEFT_PIECES, half), jnp.bfloat16),
             pltpu.SemaphoreType.DMA((2,)),
             *sems,
         ],

time: 421 us -> 400 us (0.950)
  Pallas kernels: 394 us -> 372 us
    pallas_call x1, Pallas kernels: 394 us -> 372 us  [split_shards(): pl.pallas_call(functools.partial(kernel_entry, len(shapes)), out_shape=ja...]
where the time goes in v2:
time: 400 us
  Pallas kernels  372 us (93%)
  other arithmetic  20.4 us (5%)
  local copies, waits for them, and re-layouts  6.81 us (2%)
    pallas_call x1, Pallas kernels, split_shards(): pl.pallas_call(functools.partial(kernel_entry, len(shapes)), out_shape=ja...  372 us
    mul x2, other arithmetic, sparsify(): shaped * mask[:, None, :, None].astype(matrix.dtype)  17.2 us

profile of v2, /device:TPU:3, one launch (start us, length us, event | category | flops | bytes accessed | tf_op | source)
XLA Modules:
  0.0 399.6 jit_solution(16462836556842976194)
XLA Ops:
  0.0 0.7 convert_element_type.16
  0.7 0.1 copy.6
  0.8 5.4 %mul.36 = bf16[64,128,4,128]{3,2,1,0:T(4,128)(2,1)} broadcast(bf16[64,4]{1,0:T(8,128)(2,1)S(1)} %copy.6), dimensions={0,2} | broadcast | bytes 8389120 | tf_op jit(solution)/shard_map/mul | solution.py:32
  6.2 0.0 copy-start
  6.2 9.6 %bitcast_multiply_fusion.rsrc = bf16[8192,512]{1,0:T(8,128)(2,1)} fusion(bf16[8192,512]{1,0:T(8,128)(2,1)} %param.6, bf16[1024,8,4,128]{3,2,1,0:T(4,128)(2,1)} %bitcast.14), kind=kLoop, calls=%fused_computation | loop fusion | flops 4194304 | bytes 25165824 | tf_op jit(solution)/shard_map/mul | solution.py:32
  15.8 0.0 copy-done
  15.9 0.9 mul.33
  16.7 7.6 %bitcast_multiply_fusion.1.lsrc = bf16[768,4096]{1,0:T(8,128)(2,1)} fusion(bf16[768,4096]{1,0:T(8,128)(2,1)} %param.5, bf16[96,8,32,128]{3,2,1,0:T(8,128)(2,1)S(1)} %bitcast.15), kind=kLoop, calls=%fused_computation.1 | loop fusion | flops 3145728 | bytes 18874368 | tf_op jit(solution)/shard_map/mul | solution.py:32
  24.3 0.0 copy-start.1
  24.3 372.4 %shard_map.55 = f32[768,512]{1,0:T(8,128)} custom-call(bf16[768,4096]{1,0:T(8,128)(2,1)} %bitcast_multiply_fusion.1.lsrc, bf16[8192,512]{1,0:T(8,128)(2,1)} %bitcast_multiply_fusion.rsrc), custom_call_target="tpu_custom_call" | custom-call | tf_op jit(solution)/shard_map/pallas_call | solution.py:323
  396.7 0.0 copy-done.1
  396.7 0.1 copy.7
  396.8 0.3 mul.39
  397.1 2.5 fusion
  (2 shorter events, 0.0 us)
Async XLA Ops:
  6.2 9.6 %copy-start = (s32[6,32]{1,0:T(8,128)S(1)}, s32[6,32]{1,0:T(8,128)}, u32[]{:S(2)}) copy-start(s32[6,32]{1,0:T(8,128)} %param.7) | copy-start | bytes 2308
  24.3 372.4 %copy-start.1 = (s32[6,4]{0,1:T(4,128)S(1)}, s32[6,4]{0,1:T(4,128)}, u32[]{:S(2)}) copy-start(s32[6,4]{0,1:T(4,128)} %param.9) | copy-start | bytes 292

commit v3 on v2

--- a/solution.py
+++ b/solution.py
@@ -224,6 +224,7 @@
     for j in range(LEFT_PIECES):
         arrived(left_at(1 - y, z, j), y_l, (j,))
         first_hop(False, j)
+        forward(y, 1, j)
     for j in range(LEFT_PIECES):
         forward(1 - y, 1, j)
     for j in range(LEFT_PIECES // 2, LEFT_PIECES):
@@ -234,7 +235,7 @@
             send(copy(right_at(behind, q, j), right_at(behind, q, j), x_fwd, (q, j), device(0, 1, 0, p)))
     for j in range(LEFT_PIECES // 2, LEFT_PIECES):
         detour_back(j)
-    for m, own in ((2, False), (1, True), (2, True)):
+    for m, own in ((2, False), (2, True)):
         for j in range(LEFT_PIECES):
             forward(y if own else 1 - y, m, j)
 

time: 400 us -> 398 us (level)
  no operation moved by 1% of the time
where the time goes in v3:
time: 398 us
  Pallas kernels  371 us (93%)
  other arithmetic  20.4 us (5%)
  local copies, waits for them, and re-layouts  6.81 us (2%)
    pallas_call x1, Pallas kernels, split_shards(): pl.pallas_call(functools.partial(kernel_entry, len(shapes)), out_shape=ja...  371 us
    mul x2, other arithmetic, sparsify(): shaped * mask[:, None, :, None].astype(matrix.dtype)  17.2 us

profile of v3, /device:TPU:3, one launch (start us, length us, event | category | flops | bytes accessed | tf_op | source)
XLA Modules:
  0.0 397.8 jit_solution(16997336325010671900)
XLA Ops:
  0.0 0.7 convert_element_type.16
  0.7 0.1 copy.6
  0.8 5.4 %mul.36 = bf16[64,128,4,128]{3,2,1,0:T(4,128)(2,1)} broadcast(bf16[64,4]{1,0:T(8,128)(2,1)S(1)} %copy.6), dimensions={0,2} | broadcast | bytes 8389120 | tf_op jit(solution)/shard_map/mul | solution.py:32
  6.2 0.0 copy-start
  6.2 9.6 %bitcast_multiply_fusion.rsrc = bf16[8192,512]{1,0:T(8,128)(2,1)} fusion(bf16[8192,512]{1,0:T(8,128)(2,1)} %param.6, bf16[1024,8,4,128]{3,2,1,0:T(4,128)(2,1)} %bitcast.14), kind=kLoop, calls=%fused_computation | loop fusion | flops 4194304 | bytes 25165824 | tf_op jit(solution)/shard_map/mul | solution.py:32
  15.8 0.0 copy-done
  15.9 0.9 mul.33
  16.7 7.6 %bitcast_multiply_fusion.1.lsrc = bf16[768,4096]{1,0:T(8,128)(2,1)} fusion(bf16[768,4096]{1,0:T(8,128)(2,1)} %param.5, bf16[96,8,32,128]{3,2,1,0:T(8,128)(2,1)S(1)} %bitcast.15), kind=kLoop, calls=%fused_computation.1 | loop fusion | flops 3145728 | bytes 18874368 | tf_op jit(solution)/shard_map/mul | solution.py:32
  24.3 0.0 copy-start.1
  24.3 370.5 %shard_map.55 = f32[768,512]{1,0:T(8,128)} custom-call(bf16[768,4096]{1,0:T(8,128)(2,1)} %bitcast_multiply_fusion.1.lsrc, bf16[8192,512]{1,0:T(8,128)(2,1)} %bitcast_multiply_fusion.rsrc), custom_call_target="tpu_custom_call" | custom-call | tf_op jit(solution)/shard_map/pallas_call | solution.py:324
  394.8 0.0 copy-done.1
  394.9 0.1 copy.7
  395.0 0.3 mul.39
  395.2 2.5 fusion
  (2 shorter events, 0.0 us)
Async XLA Ops:
  6.2 9.6 %copy-start = (s32[6,32]{1,0:T(8,128)S(1)}, s32[6,32]{1,0:T(8,128)}, u32[]{:S(2)}) copy-start(s32[6,32]{1,0:T(8,128)} %param.7) | copy-start | bytes 2308
  24.3 370.5 %copy-start.1 = (s32[6,4]{0,1:T(4,128)S(1)}, s32[6,4]{0,1:T(4,128)}, u32[]{:S(2)}) copy-start(s32[6,4]{0,1:T(4,128)} %param.9) | copy-start | bytes 292
